TPU v7x, 32 devices: a whole 2x2x4 slice. The times are simulated.
32 devices in a mesh: rep: 2 (over y), seq: 4 (over x, core), head: 4 (over z).
Axes of the slice: x: 2, y: 2, z: 4, core: 2. Of those that a mesh axis runs over, the one named last changes fastest.
Arguments:
- query: bfloat16 [32768, 2048], P(('rep', 'seq', 'head')), parts along dimension 0, may hold values from -6 to 6
- key: bfloat16 [32768, 2048], P(('rep', 'seq', 'head')), parts along dimension 0, may hold values from -6 to 6
- value: bfloat16 [32768, 2048], P(('rep', 'seq', 'head')), parts along dimension 0, may hold values from -6 to 6
- grad_out: bfloat16 [32768, 2048], P(('rep', 'seq', 'head')), parts along dimension 0, may hold values from -6 to 6
- level_weights: bfloat16 [32768, 128], P(('rep', 'seq', 'head')), parts along dimension 0, may hold values from 0.25 to 4
Outputs:
- attended: bfloat16 [32768, 2048], P(('rep', 'seq', 'head')), parts along dimension 0
- grad_query: bfloat16 [32768, 2048], P(('rep', 'seq', 'head')), parts along dimension 0
- grad_key: bfloat16 [32768, 2048], P(('rep', 'seq', 'head')), parts along dimension 0
- grad_value: bfloat16 [32768, 2048], P(('rep', 'seq', 'head')), parts along dimension 0
- grad_weights: bfloat16 [32768, 128], P(('rep', 'seq', 'head')), parts along dimension 0
There are 2 independent parts, one for each index of `rep`. A program takes and returns all parts, laid end to end along the dimension named above; each array names one. Nothing has to cross between parts.
All inputs are finite; a program needn't handle non-finite values.
Results may differ from a plain program's by a relative error of at most 0.0056.
Values may be sent and summed in bfloat16 or wider, within the bound.
A program may use at most 384 MiB of HBM per device.

v0:
```python
import math
import jax
import jax.numpy as jnp
from jax import lax
from jax.sharding import PartitionSpec as P

DH = 128
C = 128
LEVELS = 8


def level_scale(level):
    if level == 0:
        return 1.0 / math.sqrt(DH * C)
    return 1.0 / math.sqrt(DH * C * 2 ** (level - 1))


def bucket_matrix(count, level_bit):
    rows = jnp.arange(count, dtype=jnp.int32)[:, None]
    columns = jnp.arange(count, dtype=jnp.int32)[None, :]
    stride = 2**level_bit
    reading = rows // stride % 2 == 1
    inside = columns // stride == rows // (2 * stride) * 2
    return jnp.where(reading & inside, 1.0, 0.0).astype(jnp.float32)


def local_part(query, key, value, grad_out, level_weights):
    heads = query.shape[1] // DH
    stretches = query.shape[0] // C
    blocks = (stretches, C, heads, DH)
    query_blocks = query.reshape(blocks)
    key_blocks = key.reshape(blocks)
    value_blocks = value.reshape(blocks)
    grad_blocks = grad_out.reshape(blocks)
    weights = level_weights.reshape(stretches, C, heads, LEVELS).astype(jnp.float32)
    mask = jnp.tril(jnp.ones((C, C), jnp.float32))
    scores = jnp.einsum(
        "ntgd,nsgd->ngts", query_blocks, key_blocks, preferred_element_type=jnp.float32
    ) * (level_scale(0) * mask)
    first = jnp.transpose(weights[..., 0], (0, 2, 1))[..., None]
    probs = (first * scores).astype(jnp.bfloat16)
    attended = jnp.einsum(
        "ngts,nsgd->ntgd", probs, value_blocks, preferred_element_type=jnp.float32
    )
    grad_probs = jnp.einsum(
        "ntge,nsge->ngts", grad_blocks, value_blocks, preferred_element_type=jnp.float32
    )
    grad_levels = [jnp.transpose(jnp.sum(scores * grad_probs, axis=-1), (0, 2, 1))]
    grad_scores = (first * grad_probs * (level_scale(0) * mask)).astype(jnp.bfloat16)
    grad_query = jnp.einsum(
        "ngts,nsgd->ntgd", grad_scores, key_blocks, preferred_element_type=jnp.float32
    )
    grad_key = jnp.einsum(
        "ngts,ntgd->nsgd", grad_scores, query_blocks, preferred_element_type=jnp.float32
    )
    grad_value = jnp.einsum(
        "ngts,ntge->nsge", probs, grad_blocks, preferred_element_type=jnp.float32
    )
    states = jnp.einsum(
        "nsgd,nsge->ngde", key_blocks, value_blocks, preferred_element_type=jnp.float32
    )
    products = []
    for level in range(1, LEVELS):
        weighted = (weights[..., level : level + 1] * query_blocks).astype(jnp.bfloat16)
        products.append(
            jnp.einsum("ntgd,ntge->ngde", weighted, grad_blocks, preferred_element_type=jnp.float32)
        )
    blocks_all = (query_blocks, key_blocks, value_blocks, grad_blocks, weights)
    partial_value = (attended, grad_levels, grad_query, grad_key, grad_value)
    return (blocks_all, partial_value, states, products)


def finish(blocks_all, partial_value, states, products, cross_reads, cross_adjoint):
    query_blocks, key_blocks, value_blocks, grad_blocks, weights = blocks_all
    attended, grad_levels, grad_query, grad_key, grad_value = partial_value
    stretches = query_blocks.shape[0]
    heads = query_blocks.shape[2]
    local_bits = stretches.bit_length() - 1
    adjoint = jnp.zeros((stretches, heads, DH, DH), jnp.float32)
    for level in range(1, LEVELS):
        factor = level_scale(level)
        if level <= local_bits:
            mapping = bucket_matrix(stretches, level - 1)
            summed = jnp.einsum("ij,jgde->igde", mapping, states, precision=lax.Precision.HIGHEST)
            read_state = (factor * summed).astype(jnp.bfloat16)
            reads = jnp.einsum(
                "ntgd,ngde->ntge", query_blocks, read_state, preferred_element_type=jnp.float32
            )
            backward = jnp.einsum(
                "ntge,ngde->ntgd", grad_blocks, read_state, preferred_element_type=jnp.float32
            )
            adjoint = adjoint + factor * jnp.einsum(
                "ij,igde->jgde", mapping, products[level - 1], precision=lax.Precision.HIGHEST
            )
        else:
            index = level - 1 - local_bits
            read_state = (factor * cross_reads[index]).astype(jnp.bfloat16)
            reads = jnp.einsum(
                "ntgd,gde->ntge", query_blocks, read_state, preferred_element_type=jnp.float32
            )
            backward = jnp.einsum(
                "ntge,gde->ntgd", grad_blocks, read_state, preferred_element_type=jnp.float32
            )
            adjoint = adjoint + factor * cross_adjoint[index][None]
        weight = weights[..., level : level + 1]
        attended = attended + weight * reads
        grad_levels.append(jnp.sum(grad_blocks.astype(jnp.float32) * reads, axis=-1))
        grad_query = grad_query + weight * backward
    adjoint_low = adjoint.astype(jnp.bfloat16)
    grad_key = grad_key + jnp.einsum(
        "nsge,ngde->nsgd", value_blocks, adjoint_low, preferred_element_type=jnp.float32
    )
    grad_value = grad_value + jnp.einsum(
        "nsgd,ngde->nsge", key_blocks, adjoint_low, preferred_element_type=jnp.float32
    )

    def flatten(array, width):
        return array.reshape(stretches * C, heads * width).astype(jnp.bfloat16)

    return (
        flatten(attended, DH),
        flatten(grad_query, DH),
        flatten(grad_key, DH),
        flatten(grad_value, DH),
        flatten(jnp.stack(grad_levels, axis=-1), LEVELS),
    )


def cross_inputs(states, products, stretches, cross_bits):
    local_bits = stretches.bit_length() - 1
    cross_total = jnp.sum(states, axis=0)
    cross_products = jnp.stack(
        [jnp.sum(products[local_bits + level_bit], axis=0) for level_bit in range(cross_bits)]
    )
    return (cross_total, cross_products)


def shards(query, key, value, grad_out, level_weights):
    query, key, value, grad_out, level_weights = (
        lax.all_to_all(query, "head", split_axis=1, concat_axis=0, tiled=True),
        lax.all_to_all(key, "head", split_axis=1, concat_axis=0, tiled=True),
        lax.all_to_all(value, "head", split_axis=1, concat_axis=0, tiled=True),
        lax.all_to_all(grad_out, "head", split_axis=1, concat_axis=0, tiled=True),
        lax.all_to_all(level_weights, "head", split_axis=1, concat_axis=0, tiled=True),
    )
    blocks_all, partial_value, states, products = local_part(
        query, key, value, grad_out, level_weights
    )
    stretches = states.shape[0]
    cross_bits = lax.axis_size("seq").bit_length() - 1
    position = lax.axis_index("seq")
    cross_total, cross_products = cross_inputs(states, products, stretches, cross_bits)
    totals = lax.all_gather(cross_total[None], "seq", axis=0, tiled=True)
    sums = lax.all_gather(cross_products[None], "seq", axis=0, tiled=True)
    count = totals.shape[0]
    source = jnp.arange(count, dtype=jnp.int32)[:, None]
    powers = (2 ** jnp.arange(cross_bits, dtype=jnp.int32))[None, :]
    base = position // (2 * powers) * (2 * powers)
    owned = position // powers % 2
    lower = (source >= base) & (source < base + powers)
    upper = (source >= base + powers) & (source < base + 2 * powers)
    forward = jnp.where(lower & (owned == 1), 1.0, 0.0).astype(jnp.float32)
    backward = jnp.where(upper & (owned == 0), 1.0, 0.0).astype(jnp.float32)
    read_sum = jnp.einsum("qb,qgde->bgde", forward, totals, precision=lax.Precision.HIGHEST)
    adjoint_sum = jnp.einsum("qb,qbgde->bgde", backward, sums, precision=lax.Precision.HIGHEST)
    results = finish(blocks_all, partial_value, states, products, read_sum, adjoint_sum)
    return (
        lax.all_to_all(results[0], "head", split_axis=0, concat_axis=1, tiled=True),
        lax.all_to_all(results[1], "head", split_axis=0, concat_axis=1, tiled=True),
        lax.all_to_all(results[2], "head", split_axis=0, concat_axis=1, tiled=True),
        lax.all_to_all(results[3], "head", split_axis=0, concat_axis=1, tiled=True),
        lax.all_to_all(results[4], "head", split_axis=0, concat_axis=1, tiled=True),
    )


def solution(mesh):
    return jax.shard_map(
        shards,
        mesh=mesh,
        in_specs=(
            P(("rep", "seq", "head"), None),
            P(("rep", "seq", "head"), None),
            P(("rep", "seq", "head"), None),
            P(("rep", "seq", "head"), None),
            P(("rep", "seq", "head"), None),
        ),
        out_specs=(
            P(("rep", "seq", "head"), None),
            P(("rep", "seq", "head"), None),
            P(("rep", "seq", "head"), None),
            P(("rep", "seq", "head"), None),
            P(("rep", "seq", "head"), None),
        ),
        check_vma=False,
    )
```

profile of v0, /device:TPU:0, one launch (start us, length us, event | category | flops | bytes accessed | tf_op | source)
XLA Modules:
  0.0 1145.0 jit_solution(13611935831016947654)
XLA Ops:
  33.7 87.2 %all-to-all-done.5 = bf16[1024,4,512]{2,0,1:T(8,128)(2,1)} async-done(((bf16[1024,4,512]{2,0,1:T(8,128)(2,1)}), bf16[1024,4,512]{2,0,1:T(8,128)(2,1)}, u32[]{:S(2)}, u32[]{:S(2)}) %all-to-all-start.5) | async-done | bytes 4194336 | tf_op jit(solution)/shard_map/all_to_all | solution.py:143
  130.3 88.1 %all-to-all-done.3 = bf16[1024,4,512]{2,0,1:T(8,128)(2,1)} async-done(((bf16[1024,4,512]{2,0,1:T(8,128)(2,1)}), bf16[1024,4,512]{2,0,1:T(8,128)(2,1)}, u32[]{:S(2)}, u32[]{:S(2)}) %all-to-all-start.3) | async-done | bytes 4194336 | tf_op jit(solution)/shard_map/all_to_all | solution.py:142
  227.9 88.1 %all-to-all-done.2 = bf16[1024,4,512]{2,0,1:T(8,128)(2,1)} async-done(((bf16[1024,4,512]{2,0,1:T(8,128)(2,1)}), bf16[1024,4,512]{2,0,1:T(8,128)(2,1)}, u32[]{:S(2)}, u32[]{:S(2)}) %all-to-all-start.2) | async-done | bytes 4194336 | tf_op jit(solution)/shard_map/all_to_all | solution.py:141
  323.9 6.9 reshape.630
  330.8 6.9 reshape.629
  337.7 6.9 reshape.628
  344.6 69.0 %all-to-all-done.1 = bf16[1024,4,512]{2,0,1:T(8,128)(2,1)} async-done(((bf16[1024,4,512]{2,0,1:T(8,128)(2,1)}), bf16[1024,4,512]{2,0,1:T(8,128)(2,1)}, u32[]{:S(2)}, u32[]{:S(2)}) %all-to-all-start.1) | async-done | bytes 4194336 | tf_op jit(solution)/shard_map/all_to_all | solution.py:140
  413.6 6.9 reshape.627
  433.1 11.7 %multiply_convert_fusion.1 = bf16[32,4,128,128]{3,0,2,1:T(8,128)(2,1)S(1)} fusion(f32[32,4,128,128]{3,2,1,0:T(8,128)S(1)} %get-tuple-element.42, s32[32]{0:T(128)S(1)} %get-tuple-element.47, s32[32]{0:T(128)S(1)} %get-tuple-element.46, pred[32]{0:T(512)(128)(4,1)S(1)} %fusion.227), kind=kOutput, calls=%fused_computation.75 | convolution fusion | flops 809503744 | bytes 12583200 | tf_op jit(solution)/shard_map/ij,jgde->igde/dot_general | solution.py:84
  444.8 7.9 fusion.73
  452.7 11.9 %multiply_convert_fusion.2 = bf16[32,4,128,128]{3,0,2,1:T(8,128)(2,1)S(1)} fusion(f32[32,4,128,128]{3,2,1,0:T(8,128)S(1)} %get-tuple-element.42, s32[32]{0:T(128)S(1)} %get-tuple-element.49, s32[32]{0:T(128)S(1)} %get-tuple-element.48, pred[32]{0:T(512)(128)(4,1)S(1)} %fusion.226), kind=kOutput, calls=%fused_computation.76 | convolution fusion | flops 809503744 | bytes 12583200 | tf_op jit(solution)/shard_map/ij,jgde->igde/dot_general | solution.py:84
  466.6 7.9 fusion.77
  474.5 10.5 fusion.75
  485.0 10.9 fusion.79
  496.0 11.7 %multiply_convert_fusion.3 = bf16[32,4,128,128]{3,0,2,1:T(8,128)(2,1)S(1)} fusion(f32[32,4,128,128]{3,2,1,0:T(8,128)S(1)} %get-tuple-element.42, s32[32]{0:T(128)S(1)} %get-tuple-element.51, s32[32]{0:T(128)S(1)} %get-tuple-element.50, pred[32]{0:T(512)(128)(4,1)S(1)} %fusion.225), kind=kOutput, calls=%fused_computation.77 | convolution fusion | flops 809503744 | bytes 12583200 | tf_op jit(solution)/shard_map/ij,jgde->igde/dot_general | solution.py:84
  509.8 7.8 fusion.81
  517.6 10.6 fusion.83
  528.2 11.7 %multiply_convert_fusion.5 = bf16[32,4,128,128]{3,0,2,1:T(8,128)(2,1)S(1)} fusion(f32[32,4,128,128]{3,2,1,0:T(8,128)S(1)} %get-tuple-element.42, s32[32]{0:T(128)S(1)} %broadcast_multiply_fusion.3, pred[32]{0:T(512)(128)(4,1)S(1)} %fusion.223), kind=kOutput, calls=%fused_computation.79 | convolution fusion | flops 809503744 | bytes 12583072 | tf_op jit(solution)/shard_map/ij,jgde->igde/dot_general | solution.py:84
  539.9 7.9 fusion.89
  547.9 15.7 %multiply_convert_fusion.4 = bf16[32,4,128,128]{3,0,2,1:T(8,128)(2,1)S(1)} fusion(f32[32,4,128,128]{3,2,1,0:T(8,128)} %copy-done.9, s32[32]{0:T(128)S(1)} %get-tuple-element.53, s32[32]{0:T(128)S(1)} %get-tuple-element.52, pred[32]{0:T(512)(128)(4,1)S(1)} %fusion.224), kind=kOutput, calls=%fused_computation.78 | convolution fusion | flops 809503744 | bytes 12583200 | tf_op jit(solution)/shard_map/ij,jgde->igde/dot_general | solution.py:84
  563.7 8.0 fusion.85
  571.7 7.3 fusion.56
  579.0 13.1 %fusion.32 = f32[32,4,128,128]{3,0,2,1:T(8,128)} fusion(f32[32,4,128,128]{3,2,1,0:T(8,128)S(1)} %fusion.56, s32[32]{0:T(128)S(1)} %get-tuple-element.47, s32[32]{0:T(128)S(1)} %get-tuple-element.46, pred[32]{0:T(512)(128)(4,1)S(1)} %fusion.227), kind=kOutput, calls=%fused_computation.62 | convolution fusion | flops 805309440 | bytes 16777504 | tf_op jit(solution)/shard_map/ij,igde->jgde/dot_general | solution.py:92
  598.8 11.1 multiply_reduce_fusion
  627.5 6.9 fusion.139
  634.4 25.6 %fusion.13 = (bf16[32,128,4]{1,2,0:T(4,128)(2,1)S(1)}, bf16[32,128,4]{1,2,0:T(4,128)(2,1)}, bf16[32,128,4]{1,2,0:T(4,128)(2,1)S(1)}, bf16[32,128,4]{1,2,0:T(4,12...) fusion(bf16[32,128,4,128]{3,2,1,0:T(4,128)(2,1)S(1)} %copy-done, ...), kind=kOutput, calls=%fused_computation.27 | convolution fusion | flops 568213504 | bytes 67469312 | tf_op jit(solution)/shard_map/ntgd,gde->ntge/dot_general | solution.py:98
  673.7 26.1 %fusion.25 = bf16[32,128,4,128]{3,1,2,0:T(8,128)(2,1)S(1)} fusion(f32[4,128,32,128]{1,3,0,2:T(8,128)} %get-tuple-element.45, f32[4,128,32,128]{1,3,0,2:T(8,128)} %fusion.139, f32[32,4,128,128]{2,3,1,0:T(8,128)} %fusion.73, f32[32,4,128,128]{2,3,1,0:T(8,128)} %fusion.77, f32[32,4,128,128]{2,3,1,0:T(8,128)} %fusion.81, f32[32,4,128,128]{2,3,1,0:T(8,128)} %fusion.85, ...), kind=kOutput, calls=%fused_computation.49 | convolution fusion | flops 574619648 | bytes 76087296 | tf_op jit(solution)/shard_map/ngts,nsgd->ntgd/dot_general | solution.py:42
  705.7 7.2 convert_element_type.131
  718.8 11.9 %fusion.87 = f32[32,4,128,128]{2,3,1,0:T(8,128)} fusion(bf16[32,4,128,128]{3,0,2,1:T(8,128)(2,1)} %copy-done.15, bf16[32,128,4,128]{3,2,1,0:T(4,128)(2,1)} %reshape.630), kind=kOutput, calls=%fused_computation.123 | convolution fusion | flops 536870912 | bytes 16777216 | tf_op jit(solution)/shard_map/ntge,ngde->ntgd/dot_general | solution.py:89
  731.6 17.4 %fusion.34 = f32[32,4,128,128]{3,0,2,1:T(8,128)} fusion(f32[32,4,128,128]{3,2,1,0:T(8,128)} %fusion.58, s32[32]{0:T(128)S(1)} %copy-done.42, s32[32]{0:T(128)S(1)} %copy-done.40, pred[32]{0:T(512)(128)(4,1)S(1)} %copy-done.38), kind=kOutput, calls=%fused_computation.64 | convolution fusion | flops 805309440 | bytes 16777504 | tf_op jit(solution)/shard_map/ij,igde->jgde/dot_general | solution.py:92
  755.7 8.6 fusion.105
  777.6 21.7 %fusion.17 = bf16[32,128,4,128]{3,1,2,0:T(8,128)(2,1)} fusion(f32[4,128,32,128]{1,3,0,2:T(8,128)} %fusion.133, f32[4,128,32,128]{1,3,0,2:T(8,128)} %fusion.137, f32[32,4,128,128]{2,3,1,0:T(8,128)S(1)} %bitcast.276, f32[32,4,128,128]{2,3,1,0:T(8,128)S(1)} %bitcast.278, f32[32,4,128,128]{2,3,1,0:T(8,128)} %fusion.83, f32[32,4,128,128]{2,3,1,0:T(8,128)} %fusion.87, ...), kind=kOutput, calls=%fused_computation.34 | convolution fusion | flops 568328192 | bytes 71761920 | tf_op jit(solution)/shard_map/ntge,ngde->ntgd/dot_general | solution.py:89
  799.3 8.2 copy.351
  807.5 7.2 convert_element_type.134
  819.8 17.2 %fusion.36 = f32[32,4,128,128]{3,0,2,1:T(8,128)} fusion(f32[32,4,128,128]{3,2,1,0:T(8,128)} %fusion.60, s32[32]{0:T(128)S(1)} %copy-done.36, s32[32]{0:T(128)S(1)} %copy-done.34, pred[32]{0:T(512)(128)(4,1)S(1)} %copy-done.28), kind=kOutput, calls=%fused_computation.66 | convolution fusion | flops 805309440 | bytes 16777504 | tf_op jit(solution)/shard_map/ij,igde->jgde/dot_general | solution.py:92
  837.1 7.4 fusion.62
  844.5 13.4 %fusion.38 = f32[32,4,128,128]{3,0,2,1:T(8,128)} fusion(f32[32,4,128,128]{3,2,1,0:T(8,128)S(1)} %fusion.62, s32[32]{0:T(128)S(1)} %copy-done.32, s32[32]{0:T(128)S(1)} %copy-done.30, pred[32]{0:T(512)(128)(4,1)S(1)} %copy-done.26), kind=kOutput, calls=%fused_computation.68 | convolution fusion | flops 805309440 | bytes 16777504 | tf_op jit(solution)/shard_map/ij,igde->jgde/dot_general | solution.py:92
  857.9 6.7 fusion.64
  876.9 25.1 %add_convert_fusion = bf16[32,4,128,128]{3,0,2,1:T(8,128)(2,1)} fusion(f32[32,4,128,128]{3,0,2,1:T(8,128)} %fusion.32, f32[32,4,128,128]{3,0,2,1:T(8,128)} %fusion.34, f32[32,4,128,128]{3,0,2,1:T(8,128)} %fusion.36, f32[32,4,128,128]{3,0,2,1:T(8,128)} %fusion.38, f32[4,128,128]{2,1,0:T(8,128)S(1)} %bitcast.294, f32[4,128,128]{2,1,0:T(8,128)S(1)} %bitcast.293, ...), kind=kOutput, calls=%fused_computation.73 | convolution fusion | flops 830475264 | bytes 46661792 | tf_op jit(solution)/shard_map/ij,igde->jgde/dot_general | solution.py:92
  902.0 7.7 copy.380
  909.7 7.2 fusion.15
  922.9 7.2 convert_element_type.145
  935.4 9.4 fusion.129
  944.8 9.8 fusion.14
  954.6 8.2 copy.383
  962.8 7.2 convert_element_type.147
  970.0 57.5 %all-to-all-done.7 = bf16[4,1024,512]{2,1,0:T(8,128)(2,1)} async-done(((bf16[4,1024,512]{2,1,0:T(8,128)(2,1)}), bf16[4,1024,512]{2,1,0:T(8,128)(2,1)}, u32[]{:S(2)}, u32[]{:S(2)}) %all-to-all-start.7) | async-done | bytes 4194336 | tf_op jit(solution)/shard_map/all_to_all | solution.py:170
  1071.1 54.0 %all-to-all-done.8 = bf16[4,1024,512]{2,1,0:T(8,128)(2,1)} async-done(((bf16[4,1024,512]{2,1,0:T(8,128)(2,1)}), bf16[4,1024,512]{2,1,0:T(8,128)(2,1)}, u32[]{:S(2)}, u32[]{:S(2)}) %all-to-all-start.8) | async-done | bytes 4194336 | tf_op jit(solution)/shard_map/all_to_all | solution.py:171
  (199 shorter events, 225.2 us)
Async XLA Ops:
  9.0 15.2 %all-to-all-start = ((bf16[1024,4,32]{0,2,1:T(8,128)(2,1)}), bf16[1024,4,32]{0,2,1:T(8,128)(2,1)S(1)}, u32[]{:S(2)}, u32[]{:S(2)}) async-start(bf16[1024,4,32]{0,2,1:T(8,128)(2,1)} %bitcast), calls=%async_computation | async-start | bytes 524288 | tf_op jit(solution)/shard_map/all_to_all | solution.py:144
  24.2 96.7 %all-to-all-start.5 = ((bf16[1024,4,512]{2,0,1:T(8,128)(2,1)}), bf16[1024,4,512]{2,0,1:T(8,128)(2,1)}, u32[]{:S(2)}, u32[]{:S(2)}) async-start(bf16[1024,4,512]{2,0,1:T(8,128)(2,1)} %bitcast.280), calls=%async_computation.5 | async-start | bytes 8388608 | tf_op jit(solution)/shard_map/all_to_all | solution.py:143
  120.9 97.5 %all-to-all-start.3 = ((bf16[1024,4,512]{2,0,1:T(8,128)(2,1)}), bf16[1024,4,512]{2,0,1:T(8,128)(2,1)}, u32[]{:S(2)}, u32[]{:S(2)}) async-start(bf16[1024,4,512]{2,0,1:T(8,128)(2,1)} %bitcast.281), calls=%async_computation.3 | async-start | bytes 8388608 | tf_op jit(solution)/shard_map/all_to_all | solution.py:142
  218.4 97.6 %all-to-all-start.2 = ((bf16[1024,4,512]{2,0,1:T(8,128)(2,1)}), bf16[1024,4,512]{2,0,1:T(8,128)(2,1)}, u32[]{:S(2)}, u32[]{:S(2)}) async-start(bf16[1024,4,512]{2,0,1:T(8,128)(2,1)} %bitcast.282), calls=%async_computation.2 | async-start | bytes 8388608 | tf_op jit(solution)/shard_map/all_to_all | solution.py:141
  316.0 97.6 %all-to-all-start.1 = ((bf16[1024,4,512]{2,0,1:T(8,128)(2,1)}), bf16[1024,4,512]{2,0,1:T(8,128)(2,1)}, u32[]{:S(2)}, u32[]{:S(2)}) async-start(bf16[1024,4,512]{2,0,1:T(8,128)(2,1)} %bitcast.279), calls=%async_computation.1 | async-start | bytes 8388608 | tf_op jit(solution)/shard_map/all_to_all | solution.py:140
  320.9 301.8 %all-gather.5.cloned.1.call-start = ((), (), s32[]{:S(2)}) async-start(), calls=%async_computation.10 | async-start | bytes 1310720 | tf_op jit(solution)/shard_map/all_gather | solution.py:153
  321.5 206.7 %copy-start.43 = (s32[32]{0:T(128)}, s32[32]{0:T(128)S(1)}, u32[]{:S(2)}) copy-start(s32[32]{0:T(128)S(1)} %broadcast_multiply_fusion.3) | copy-start | bytes 388
  321.5 206.7 %copy-start.45 = (pred[32]{0:T(512)(128)(4,1)}, pred[32]{0:T(512)(128)(4,1)S(1)}, u32[]{:S(2)}) copy-start(pred[32]{0:T(512)(128)(4,1)S(1)} %fusion.223) | copy-start | bytes 100
  321.6 131.1 %copy-start.37 = (pred[32]{0:T(512)(128)(4,1)}, pred[32]{0:T(512)(128)(4,1)S(1)}, u32[]{:S(2)}) copy-start(pred[32]{0:T(512)(128)(4,1)S(1)} %fusion.226) | copy-start | bytes 100
  321.6 174.4 %copy-start.27 = (pred[32]{0:T(512)(128)(4,1)}, pred[32]{0:T(512)(128)(4,1)S(1)}, u32[]{:S(2)}) copy-start(pred[32]{0:T(512)(128)(4,1)S(1)} %fusion.225) | copy-start | bytes 100
  321.6 226.3 %copy-start.25 = (pred[32]{0:T(512)(128)(4,1)}, pred[32]{0:T(512)(128)(4,1)S(1)}, u32[]{:S(2)}) copy-start(pred[32]{0:T(512)(128)(4,1)S(1)} %fusion.224) | copy-start | bytes 100
  322.1 130.6 %copy-start.39 = (s32[32]{0:T(128)}, s32[32]{0:T(128)S(1)}, u32[]{:S(2)}) copy-start(s32[32]{0:T(128)S(1)} %get-tuple-element.48) | copy-start | bytes 388
  322.1 130.6 %copy-start.41 = (s32[32]{0:T(128)}, s32[32]{0:T(128)S(1)}, u32[]{:S(2)}) copy-start(s32[32]{0:T(128)S(1)} %get-tuple-element.49) | copy-start | bytes 388
  322.1 173.9 %copy-start.33 = (s32[32]{0:T(128)}, s32[32]{0:T(128)S(1)}, u32[]{:S(2)}) copy-start(s32[32]{0:T(128)S(1)} %get-tuple-element.50) | copy-start | bytes 388
  322.1 173.9 %copy-start.35 = (s32[32]{0:T(128)}, s32[32]{0:T(128)S(1)}, u32[]{:S(2)}) copy-start(s32[32]{0:T(128)S(1)} %get-tuple-element.51) | copy-start | bytes 388
  322.1 225.7 %copy-start.29 = (s32[32]{0:T(128)}, s32[32]{0:T(128)S(1)}, u32[]{:S(2)}) copy-start(s32[32]{0:T(128)S(1)} %get-tuple-element.52) | copy-start | bytes 388
  322.1 225.7 %copy-start.31 = (s32[32]{0:T(128)}, s32[32]{0:T(128)S(1)}, u32[]{:S(2)}) copy-start(s32[32]{0:T(128)S(1)} %get-tuple-element.53) | copy-start | bytes 388
  426.8 101.4 %copy-start.9 = (f32[32,4,128,128]{3,2,1,0:T(8,128)}, f32[32,4,128,128]{3,2,1,0:T(8,128)S(1)}, u32[]{:S(2)}) copy-start(f32[32,4,128,128]{3,2,1,0:T(8,128)S(1)} %get-tuple-element.42) | copy-start | bytes 25165828
  444.8 7.9 copy-start.16
  466.6 7.9 copy-start
  539.9 7.9 copy-start.13
  547.9 15.7 %copy-start.6 = (bf16[32,128,4,128]{3,2,1,0:T(4,128)(2,1)S(1)}, bf16[32,128,4,128]{3,2,1,0:T(4,128)(2,1)}, u32[]{:S(2)}) copy-start(bf16[32,128,4,128]{3,2,1,0:T(4,128)(2,1)} %reshape.627) | copy-start | bytes 12582916
  563.6 8.0 copy-start.15
  563.6 8.0 copy-start.1
  669.9 43.0 %all-to-all-start.9 = ((bf16[4,1024,32]{1,2,0:T(8,128)(2,1)}), bf16[4,1024,32]{1,2,0:T(8,128)(2,1)S(1)}, u32[]{:S(2)}, u32[]{:S(2)}) async-start(bf16[4,1024,32]{1,2,0:T(8,128)(2,1)} %copy.387), calls=%async_computation.9 | async-start | bytes 524288 | tf_op jit(solution)/shard_map/all_to_all | solution.py:172
  713.6 101.1 %all-to-all-start.4 = ((bf16[4,1024,512]{2,1,0:T(8,128)(2,1)}), bf16[4,1024,512]{2,1,0:T(8,128)(2,1)}, u32[]{:S(2)}, u32[]{:S(2)}) async-start(bf16[4,1024,512]{2,1,0:T(8,128)(2,1)} %convert_element_type.131), calls=%async_computation.4 | async-start | bytes 8388608 | tf_op jit(solution)/shard_map/all_to_all | solution.py:168
  718.7 12.0 %copy-start.22 = (f32[1,4,128,128]{3,2,1,0:T(8,128)S(1)}, f32[1,4,128,128]{3,2,1,0:T(8,128)}, u32[]{:S(2)}) copy-start(f32[1,4,128,128]{3,2,1,0:T(8,128)} %fusion.124) | copy-start | bytes 786436
  718.7 12.0 %copy-start.23 = (f32[1,4,128,128]{3,2,1,0:T(8,128)S(1)}, f32[1,4,128,128]{3,2,1,0:T(8,128)}, u32[]{:S(2)}) copy-start(f32[1,4,128,128]{3,2,1,0:T(8,128)} %fusion.121) | copy-start | bytes 786436
  718.7 12.8 %copy-start.38 = (pred[32]{0:T(512)(128)(4,1)S(1)}, pred[32]{0:T(512)(128)(4,1)}, u32[]{:S(2)}) copy-start(pred[32]{0:T(512)(128)(4,1)} %copy-done.37) | copy-start | bytes 100
  718.7 12.8 %copy-start.40 = (s32[32]{0:T(128)S(1)}, s32[32]{0:T(128)}, u32[]{:S(2)}) copy-start(s32[32]{0:T(128)} %copy-done.39) | copy-start | bytes 388
  718.7 12.8 %copy-start.42 = (s32[32]{0:T(128)S(1)}, s32[32]{0:T(128)}, u32[]{:S(2)}) copy-start(s32[32]{0:T(128)} %copy-done.41) | copy-start | bytes 388
  718.7 150.7 %all-gather.7.cloned.1.call-start = ((), (), s32[]{:S(2)}) async-start(), calls=%async_computation.11 | async-start | bytes 2621440 | tf_op jit(solution)/shard_map/all_gather | solution.py:154
  731.5 17.5 %copy-start.3 = (bf16[32,128,4,128]{3,2,1,0:T(4,128)(2,1)S(1)}, bf16[32,128,4,128]{3,2,1,0:T(4,128)(2,1)}, u32[]{:S(2)}) copy-start(bf16[32,128,4,128]{3,2,1,0:T(4,128)(2,1)} %reshape.630) | copy-start | bytes 12582916
  731.6 17.5 %copy-start.7 = (bf16[32,128,4,128]{3,2,1,0:T(4,128)(2,1)S(1)}, bf16[32,128,4,128]{3,2,1,0:T(4,128)(2,1)}, u32[]{:S(2)}) copy-start(bf16[32,128,4,128]{3,2,1,0:T(4,128)(2,1)} %reshape.627) | copy-start | bytes 12582916
  755.7 8.6 copy-start.19
  764.3 11.0 slice-start.2
  764.3 11.0 slice-start.4
  769.8 7.8 copy-start.14
  814.7 115.3 %all-to-all-start.6 = ((bf16[4,1024,512]{2,1,0:T(8,128)(2,1)}), bf16[4,1024,512]{2,1,0:T(8,128)(2,1)}, u32[]{:S(2)}, u32[]{:S(2)}) async-start(bf16[4,1024,512]{2,1,0:T(8,128)(2,1)} %convert_element_type.134), calls=%async_computation.6 | async-start | bytes 8388608 | tf_op jit(solution)/shard_map/all_to_all | solution.py:169
  819.8 17.3 %copy-start.4 = (bf16[32,128,4,128]{3,2,1,0:T(4,128)(2,1)S(1)}, bf16[32,128,4,128]{3,2,1,0:T(4,128)(2,1)}, u32[]{:S(2)}) copy-start(bf16[32,128,4,128]{3,2,1,0:T(4,128)(2,1)} %reshape.630) | copy-start | bytes 12582916
  819.8 17.3 %copy-start.8 = (bf16[32,128,4,128]{3,2,1,0:T(4,128)(2,1)S(1)}, bf16[32,128,4,128]{3,2,1,0:T(4,128)(2,1)}, u32[]{:S(2)}) copy-start(bf16[32,128,4,128]{3,2,1,0:T(4,128)(2,1)} %reshape.627) | copy-start | bytes 12582916
  844.5 20.2 %slice-start = ((s8[8388608]{0:T(1024)(128)(4,1)}), s8[4194304]{0:T(1024)(128)(4,1)S(1)}, s32[]{:S(2)}) async-start(s8[8388608]{0:T(1024)(128)(4,1)} %bitcast.273), calls=%async_computation.12 | async-start | bytes 8388608
  869.4 7.5 copy-start.44
  869.4 7.5 copy-start.46
  930.0 97.5 %all-to-all-start.7 = ((bf16[4,1024,512]{2,1,0:T(8,128)(2,1)}), bf16[4,1024,512]{2,1,0:T(8,128)(2,1)}, u32[]{:S(2)}, u32[]{:S(2)}) async-start(bf16[4,1024,512]{2,1,0:T(8,128)(2,1)} %convert_element_type.145), calls=%async_computation.7 | async-start | bytes 8388608 | tf_op jit(solution)/shard_map/all_to_all | solution.py:170
  935.4 9.4 copy-start.12
  970.0 62.4 %copy-start.21 = (bf16[4,1024,32]{1,2,0:T(8,128)(2,1)S(1)}, bf16[4,1024,32]{1,2,0:T(8,128)(2,1)}, u32[]{:S(2)}) copy-start(bf16[4,1024,32]{1,2,0:T(8,128)(2,1)} %copy-done.20) | copy-start | bytes 786436
  1027.5 97.6 %all-to-all-start.8 = ((bf16[4,1024,512]{2,1,0:T(8,128)(2,1)}), bf16[4,1024,512]{2,1,0:T(8,128)(2,1)}, u32[]{:S(2)}, u32[]{:S(2)}) async-start(bf16[4,1024,512]{2,1,0:T(8,128)(2,1)} %convert_element_type.147), calls=%async_computation.8 | async-start | bytes 8388608 | tf_op jit(solution)/shard_map/all_to_all | solution.py:171
  (17 other events, 91.8 us)
Sparse Core Ops, SparseCore 0:
  548.0 15.8 all-gather.4
  731.6 24.0 all-gather.6
where the time goes:
time: 1150 us; the launch traced here: 1140 us
  waiting for transfers between devices  448 us (39%)
  matrix products  444 us (39%)
  local copies, waits for them, and re-layouts  183 us (16%)
  starting transfers between devices  50.6 us (4%)
  between operations  15.2 us (1%)
    all_to_all x1, waiting for transfers between devices, shards(): lax.all_to_all(value, 'head', split_axis=1, concat_axis=0, tiled=True)  88.1 us
    all_to_all x1, waiting for transfers between devices, shards(): lax.all_to_all(key, 'head', split_axis=1, concat_axis=0, tiled=True)  88.1 us
    all_to_all x1, waiting for transfers between devices, shards(): lax.all_to_all(grad_out, 'head', split_axis=1, concat_axis=0, tiled=True)  87.2 us
    dot_general x5, matrix products, finish(): jnp.einsum('ij,igde->jgde', mapping, products[level - 1], precision=lax.P...  86.3 us
    all_to_all x1, waiting for transfers between devices, shards(): lax.all_to_all(query, 'head', split_axis=1, concat_axis=0, tiled=True)  69 us
    dot_general x5, matrix products, finish(): jnp.einsum('ntge,ngde->ntgd', grad_blocks, read_state, preferred_element_...  65.6 us
    dot_general x5, matrix products, finish(): jnp.einsum('ij,jgde->igde', mapping, states, precision=lax.Precision.HIGH...  62.7 us
    convert_element_type x10, local copies, waits for them, and re-layouts, flatten(): return array.reshape(stretches * C, heads * width).astype(jnp.bfloat16)  57.8 us
  transfers between devices with their start and end apart: 12, of which 7 were waited for; matrix products, arithmetic and copies ran while one was open for 38% of the time, Pallas kernels for 0%

commit v1 on v0

--- a/solution.py
+++ b/solution.py
@@ -7,6 +7,13 @@
 DH = 128
 C = 128
 LEVELS = 8
+
+
+def swap_blocks(x, axis, split, join):
+    peers = lax.axis_size(axis)
+    parts = jnp.stack(jnp.split(x, peers, axis=split), axis=0)
+    parts = lax.all_to_all(parts, axis, split_axis=0, concat_axis=0)
+    return jnp.concatenate(parts, axis=join)
 
 
 def level_scale(level):
@@ -139,7 +146,7 @@
     query, key, value, grad_out, level_weights = (
         lax.all_to_all(query, "head", split_axis=1, concat_axis=0, tiled=True),
         lax.all_to_all(key, "head", split_axis=1, concat_axis=0, tiled=True),
-        lax.all_to_all(value, "head", split_axis=1, concat_axis=0, tiled=True),
+        swap_blocks(value, "head", 1, 0),
         lax.all_to_all(grad_out, "head", split_axis=1, concat_axis=0, tiled=True),
         lax.all_to_all(level_weights, "head", split_axis=1, concat_axis=0, tiled=True),
     )

time: 1150 us -> 1110 us (0.965)
  matrix products: 444 us -> 402 us
  local copies, waits for them, and re-layouts: 183 us -> 198 us
    all_to_all x1, waiting for transfers between devices: 88.1 us -> 51.7 us  [swap_blocks(): parts = lax.all_to_all(parts, axis, split_axis=0, concat_axis=0)]
    dot_general x5, matrix products: 65.6 us -> 42.6 us  [finish(): jnp.einsum('ntge,ngde->ntgd', grad_blocks, read_state, preferred_element_...]
    all_to_all x1, waiting for transfers between devices: 69 us -> 88.1 us  [shards(): lax.all_to_all(query, 'head', split_axis=1, concat_axis=0, tiled=True)]
    dot_general x5, matrix products: 62.7 us -> 44 us  [finish(): jnp.einsum('ij,jgde->igde', mapping, states, precision=lax.Precision.HIGH...]
    dot_general x7, matrix products: 46.9 us -> 31.1 us  [local_part(): jnp.einsum('ntgd,ntge->ngde', weighted, grad_blocks, preferred_element_ty...]
    dot_general x2, matrix products: 11 us -> 26.4 us  [finish(): jnp.einsum('ntge,gde->ntgd', grad_blocks, read_state, preferred_element_t...]
    unnamed x119 -> x125, local copies, waits for them, and re-layouts: 43.7 us -> 32.9 us
  transfers between devices with their start and end apart: 12 -> 12, of which waited for: 7 -> 8; matrix products, arithmetic and copies ran while one was open for 38% -> 41% of each run, Pallas kernels for 0% -> 0%
where the time goes in v1:
time: 1110 us
  waiting for transfers between devices  438 us (39%)
  matrix products  402 us (36%)
  local copies, waits for them, and re-layouts  198 us (18%)
  starting transfers between devices  49.7 us (4%)
  between operations  15.2 us (1%)
    all_to_all x1, waiting for transfers between devices, shards(): lax.all_to_all(query, 'head', split_axis=1, concat_axis=0, tiled=True)  88.1 us
    all_to_all x1, waiting for transfers between devices, shards(): lax.all_to_all(key, 'head', split_axis=1, concat_axis=0, tiled=True)  87.9 us
    all_to_all x1, waiting for transfers between devices, shards(): lax.all_to_all(grad_out, 'head', split_axis=1, concat_axis=0, tiled=True)  87.2 us
    dot_general x5, matrix products, finish(): jnp.einsum('ij,igde->jgde', mapping, products[level - 1], precision=lax.P...  86.1 us
    convert_element_type x10, local copies, waits for them, and re-layouts, flatten(): return array.reshape(stretches * C, heads * width).astype(jnp.bfloat16)  59 us
    all_to_all x1, waiting for transfers between devices, shards(): lax.all_to_all(results[2], 'head', split_axis=0, concat_axis=1, tiled=True)  56.3 us
    all_to_all x1, waiting for transfers between devices, shards(): lax.all_to_all(results[3], 'head', split_axis=0, concat_axis=1, tiled=True)  54 us
    all_to_all x1, waiting for transfers between devices, swap_blocks(): parts = lax.all_to_all(parts, axis, split_axis=0, concat_axis=0)  51.7 us
  transfers between devices with their start and end apart: 12, of which 8 were waited for; matrix products, arithmetic and copies ran while one was open for 41% of the time, Pallas kernels for 0%

profile of v1, /device:TPU:0, one launch (start us, length us, event | category | flops | bytes accessed | tf_op | source)
XLA Modules:
  0.0 1108.1 jit_solution(16490683352123702502)
XLA Ops:
  33.6 87.2 %all-to-all-done.5 = bf16[1024,4,512]{2,0,1:T(8,128)(2,1)} async-done(((bf16[1024,4,512]{2,0,1:T(8,128)(2,1)}), bf16[1024,4,512]{2,0,1:T(8,128)(2,1)}, u32[]{:S(2)}, u32[]{:S(2)}) %all-to-all-start.5) | async-done | bytes 4194336 | tf_op jit(solution)/shard_map/all_to_all | solution.py:150
  130.4 88.1 %all-to-all-done.2 = bf16[1024,4,512]{2,0,1:T(8,128)(2,1)} async-done(((bf16[1024,4,512]{2,0,1:T(8,128)(2,1)}), bf16[1024,4,512]{2,0,1:T(8,128)(2,1)}, u32[]{:S(2)}, u32[]{:S(2)}) %all-to-all-start.2) | async-done | bytes 4194336 | tf_op jit(solution)/shard_map/all_to_all | solution.py:147
  228.1 87.9 %all-to-all-done.3 = bf16[1024,4,512]{2,0,1:T(8,128)(2,1)} async-done(((bf16[1024,4,512]{2,0,1:T(8,128)(2,1)}), bf16[1024,4,512]{2,0,1:T(8,128)(2,1)}, u32[]{:S(2)}, u32[]{:S(2)}) %all-to-all-start.3) | async-done | bytes 4194336 | tf_op jit(solution)/shard_map/all_to_all | solution.py:148
  333.6 7.2 copy.340
  347.7 7.2 copy.316
  361.9 51.7 %all-to-all-done = bf16[4,1024,512]{2,1,0:T(8,128)(2,1)} async-done(((bf16[4,1024,512]{2,1,0:T(8,128)(2,1)}), bf16[4,1024,512]{2,1,0:T(8,128)(2,1)}, u32[]{:S(2)}, u32[]{:S(2)}) %all-to-all-start) | async-done | bytes 4194336 | tf_op jit(solution)/shard_map/all_to_all | solution.py:15
  420.4 8.5 fusion.243
  428.9 10.3 copy.260
  439.2 8.2 fusion.97
  447.4 8.6 multiply_convert_fusion.1
  456.0 8.0 fusion.70
  464.1 8.7 multiply_convert_fusion
  472.8 8.1 fusion.66
  480.9 7.7 fusion.68
  488.7 7.9 fusion.72
  496.6 8.2 multiply_convert_fusion.2
  504.7 8.1 fusion.74
  512.9 7.8 fusion.76
  520.6 8.7 multiply_convert_fusion.3
  529.3 8.1 fusion.78
  537.4 7.7 fusion.80
  546.1 9.9 multiply_convert_fusion.4
  558.0 8.2 fusion.82
  583.5 13.2 %fusion.35 = f32[32,4,128,128]{3,0,2,1:T(8,128)} fusion(f32[32,4,128,128]{3,2,1,0:T(8,128)S(1)} %fusion.49, s32[32]{0:T(128)S(1)} %fusion.209, s32[32]{0:T(128)S(1)} %and_select_fusion.7, pred[32]{0:T(512)(128)(4,1)S(1)} %fusion.208), kind=kOutput, calls=%fused_computation.67 | convolution fusion | flops 805309440 | bytes 16777504 | tf_op jit(solution)/shard_map/ij,igde->jgde/dot_general | solution.py:99
  600.9 7.2 fusion.120
  608.1 23.2 %fusion.13 = (bf16[32,128,4]{1,2,0:T(4,128)(2,1)S(1)}, bf16[32,128,4]{1,2,0:T(4,128)(2,1)S(1)}, bf16[32,128,4]{1,2,0:T(4,128)(2,1)S(1)}, bf16[32,128,4]{1,2,0:T(...) fusion(bf16[32,128,4,128]{1,3,2,0:T(8,128)(2,1)S(1)} %copy-done, ...), kind=kOutput, calls=%fused_computation.27 | convolution fusion | flops 568213504 | bytes 67469312 | tf_op jit(solution)/shard_map/ntgd,gde->ntge/dot_general | solution.py:105
  635.9 25.9 %fusion.28 = bf16[32,128,4,128]{1,3,2,0:T(8,128)(2,1)} fusion(f32[4,128,32,128]{3,1,0,2:T(8,128)} %get-tuple-element.49, f32[4,128,32,128]{3,1,0,2:T(8,128)} %fusion.120, f32[32,4,128,128]{3,2,1,0:T(8,128)} %fusion.66, f32[32,4,128,128]{3,2,1,0:T(8,128)} %fusion.70, f32[32,4,128,128]{3,2,1,0:T(8,128)} %fusion.74, f32[32,4,128,128]{3,2,1,0:T(8,128)} %fusion.78, ...), kind=kOutput, calls=%fused_computation.54 | convolution fusion | flops 574619648 | bytes 76087296 | tf_op jit(solution)/shard_map/ngts,nsgd->ntgd/dot_general | solution.py:49
  661.8 7.5 copy.293
  669.3 7.2 convert_element_type.131
  681.5 11.5 %fusion.84 = f32[32,4,128,128]{3,2,1,0:T(8,128)} fusion(bf16[32,128,4,128]{1,3,2,0:T(8,128)(2,1)} %copy.340, bf16[32,4,128,128]{3,0,2,1:T(8,128)(2,1)} %copy-done.13), kind=kOutput, calls=%fused_computation.120 | convolution fusion | flops 536870912 | bytes 16777216 | tf_op jit(solution)/shard_map/ntge,ngde->ntgd/dot_general | solution.py:96
  696.1 13.2 %fusion.37 = f32[32,4,128,128]{3,0,2,1:T(8,128)} fusion(f32[32,4,128,128]{3,2,1,0:T(8,128)S(1)} %fusion.51, s32[32]{0:T(128)S(1)} %copy-done.47, s32[32]{0:T(128)S(1)} %copy-done.49, pred[32]{0:T(512)(128)(4,1)S(1)} %copy-done.51), kind=kOutput, calls=%fused_computation.69 | convolution fusion | flops 805309440 | bytes 16777504 | tf_op jit(solution)/shard_map/ij,igde->jgde/dot_general | solution.py:99
  715.6 8.6 fusion.94
  728.8 21.9 %fusion.17 = bf16[32,128,4,128]{1,3,2,0:T(8,128)(2,1)} fusion(f32[4,128,32,128]{3,1,0,2:T(8,128)} %fusion.118, f32[32,4,128,128]{3,2,1,0:T(8,128)} %fusion.68, f32[32,4,128,128]{3,2,1,0:T(8,128)} %fusion.72, f32[32,4,128,128]{3,2,1,0:T(8,128)} %fusion.76, f32[32,4,128,128]{3,2,1,0:T(8,128)} %fusion.80, f32[32,4,128,128]{3,2,1,0:T(8,128)} %fusion.84, ...), kind=kOutput, calls=%fused_computation.34 | convolution fusion | flops 568328192 | bytes 67698688 | tf_op jit(solution)/shard_map/ntge,gde->ntgd/dot_general | solution.py:108
  750.6 7.8 copy.313
  758.4 7.2 convert_element_type.134
  765.7 8.1 all-to-all-done.4
  778.7 17.3 %fusion.39 = f32[32,4,128,128]{3,0,2,1:T(8,128)} fusion(f32[32,4,128,128]{3,2,1,0:T(8,128)} %fusion.53, s32[32]{0:T(128)S(1)} %copy-done.41, s32[32]{0:T(128)S(1)} %copy-done.43, pred[32]{0:T(512)(128)(4,1)S(1)} %copy-done.45), kind=kOutput, calls=%fused_computation.71 | convolution fusion | flops 805309440 | bytes 16777504 | tf_op jit(solution)/shard_map/ij,igde->jgde/dot_general | solution.py:99
  802.4 17.4 %fusion.41 = f32[32,4,128,128]{3,0,2,1:T(8,128)} fusion(f32[32,4,128,128]{3,2,1,0:T(8,128)} %fusion.55, s32[32]{0:T(128)S(1)} %copy-done.35, s32[32]{0:T(128)S(1)} %copy-done.37, pred[32]{0:T(512)(128)(4,1)S(1)} %copy-done.39), kind=kOutput, calls=%fused_computation.73 | convolution fusion | flops 805309440 | bytes 16777504 | tf_op jit(solution)/shard_map/ij,igde->jgde/dot_general | solution.py:99
  840.0 25.1 %add_convert_fusion = bf16[32,4,128,128]{3,0,2,1:T(8,128)(2,1)} fusion(f32[32,4,128,128]{3,0,2,1:T(8,128)} %fusion.35, f32[32,4,128,128]{3,0,2,1:T(8,128)} %fusion.37, f32[32,4,128,128]{3,0,2,1:T(8,128)} %fusion.39, f32[32,4,128,128]{3,0,2,1:T(8,128)} %fusion.41, f32[4,128,128]{2,1,0:T(8,128)S(1)} %bitcast.328, f32[4,128,128]{2,1,0:T(8,128)S(1)} %bitcast.327, ...), kind=kOutput, calls=%fused_computation.77 | convolution fusion | flops 830475264 | bytes 46661792 | tf_op jit(solution)/shard_map/ij,igde->jgde/dot_general | solution.py:99
  865.1 7.5 copy.335
  872.6 7.1 fusion.15
  885.7 7.2 convert_element_type.145
  898.3 11.0 fusion.109
  909.3 9.8 fusion.14
  919.1 8.2 copy.338
  927.3 7.2 convert_element_type.147
  934.5 56.3 %all-to-all-done.7 = bf16[4,1024,512]{2,1,0:T(8,128)(2,1)} async-done(((bf16[4,1024,512]{2,1,0:T(8,128)(2,1)}), bf16[4,1024,512]{2,1,0:T(8,128)(2,1)}, u32[]{:S(2)}, u32[]{:S(2)}) %all-to-all-start.7) | async-done | bytes 4194336 | tf_op jit(solution)/shard_map/all_to_all | solution.py:177
  1034.4 54.0 %all-to-all-done.8 = bf16[4,1024,512]{2,1,0:T(8,128)(2,1)} async-done(((bf16[4,1024,512]{2,1,0:T(8,128)(2,1)}), bf16[4,1024,512]{2,1,0:T(8,128)(2,1)}, u32[]{:S(2)}, u32[]{:S(2)}) %all-to-all-start.8) | async-done | bytes 4194336 | tf_op jit(solution)/shard_map/all_to_all | solution.py:178
  (213 shorter events, 230.6 us)
Async XLA Ops:
  9.0 15.2 %all-to-all-start.1 = ((bf16[1024,4,32]{0,2,1:T(8,128)(2,1)}), bf16[1024,4,32]{0,2,1:T(8,128)(2,1)S(1)}, u32[]{:S(2)}, u32[]{:S(2)}) async-start(bf16[1024,4,32]{0,2,1:T(8,128)(2,1)} %bitcast.4), calls=%async_computation.1 | async-start | bytes 524288 | tf_op jit(solution)/shard_map/all_to_all | solution.py:151
  24.2 96.7 %all-to-all-start.5 = ((bf16[1024,4,512]{2,0,1:T(8,128)(2,1)}), bf16[1024,4,512]{2,0,1:T(8,128)(2,1)}, u32[]{:S(2)}, u32[]{:S(2)}) async-start(bf16[1024,4,512]{2,0,1:T(8,128)(2,1)} %bitcast.316), calls=%async_computation.5 | async-start | bytes 8388608 | tf_op jit(solution)/shard_map/all_to_all | solution.py:150
  120.9 97.6 %all-to-all-start.2 = ((bf16[1024,4,512]{2,0,1:T(8,128)(2,1)}), bf16[1024,4,512]{2,0,1:T(8,128)(2,1)}, u32[]{:S(2)}, u32[]{:S(2)}) async-start(bf16[1024,4,512]{2,0,1:T(8,128)(2,1)} %bitcast.317), calls=%async_computation.2 | async-start | bytes 8388608 | tf_op jit(solution)/shard_map/all_to_all | solution.py:147
  218.5 97.5 %all-to-all-start.3 = ((bf16[1024,4,512]{2,0,1:T(8,128)(2,1)}), bf16[1024,4,512]{2,0,1:T(8,128)(2,1)}, u32[]{:S(2)}, u32[]{:S(2)}) async-start(bf16[1024,4,512]{2,0,1:T(8,128)(2,1)} %bitcast.315), calls=%async_computation.3 | async-start | bytes 8388608 | tf_op jit(solution)/shard_map/all_to_all | solution.py:148
  316.0 97.6 %all-to-all-start = ((bf16[4,1024,512]{2,1,0:T(8,128)(2,1)}), bf16[4,1024,512]{2,1,0:T(8,128)(2,1)}, u32[]{:S(2)}, u32[]{:S(2)}) async-start(bf16[4,1024,512]{2,1,0:T(8,128)(2,1)} %pad_maximum_fusion), calls=%async_computation | async-start | bytes 8388608 | tf_op jit(solution)/shard_map/all_to_all | solution.py:15
  320.9 275.9 %all-gather.5.cloned.1.call-start = ((), (), s32[]{:S(2)}) async-start(), calls=%async_computation.10 | async-start | bytes 1310720 | tf_op jit(solution)/shard_map/all_gather | solution.py:160
  321.2 199.5 %copy-start.34 = (s32[32]{0:T(128)}, s32[32]{0:T(128)S(1)}, u32[]{:S(2)}) copy-start(s32[32]{0:T(128)S(1)} %broadcast_multiply_fusion.2) | copy-start | bytes 388
  321.2 199.4 %copy-start.36 = (s32[32]{0:T(128)}, s32[32]{0:T(128)S(1)}, u32[]{:S(2)}) copy-start(s32[32]{0:T(128)S(1)} %and_select_fusion.13) | copy-start | bytes 388
  321.2 199.4 %copy-start.38 = (pred[32]{0:T(512)(128)(4,1)}, pred[32]{0:T(512)(128)(4,1)S(1)}, u32[]{:S(2)}) copy-start(pred[32]{0:T(512)(128)(4,1)S(1)} %fusion.205) | copy-start | bytes 100
  321.3 175.3 %copy-start.40 = (s32[32]{0:T(128)}, s32[32]{0:T(128)S(1)}, u32[]{:S(2)}) copy-start(s32[32]{0:T(128)S(1)} %broadcast_multiply_fusion.1) | copy-start | bytes 388
  321.3 175.3 %copy-start.42 = (s32[32]{0:T(128)}, s32[32]{0:T(128)S(1)}, u32[]{:S(2)}) copy-start(s32[32]{0:T(128)S(1)} %and_select_fusion.11) | copy-start | bytes 388
  321.3 175.3 %copy-start.44 = (pred[32]{0:T(512)(128)(4,1)}, pred[32]{0:T(512)(128)(4,1)S(1)}, u32[]{:S(2)}) copy-start(pred[32]{0:T(512)(128)(4,1)S(1)} %fusion.206) | copy-start | bytes 100
  321.3 126.1 %copy-start.46 = (s32[32]{0:T(128)}, s32[32]{0:T(128)S(1)}, u32[]{:S(2)}) copy-start(s32[32]{0:T(128)S(1)} %broadcast_multiply_fusion) | copy-start | bytes 388
  321.3 126.1 %copy-start.48 = (s32[32]{0:T(128)}, s32[32]{0:T(128)S(1)}, u32[]{:S(2)}) copy-start(s32[32]{0:T(128)S(1)} %and_select_fusion.9) | copy-start | bytes 388
  321.4 126.0 %copy-start.50 = (pred[32]{0:T(512)(128)(4,1)}, pred[32]{0:T(512)(128)(4,1)S(1)}, u32[]{:S(2)}) copy-start(pred[32]{0:T(512)(128)(4,1)S(1)} %fusion.207) | copy-start | bytes 100
  321.4 224.6 %copy-start.30 = (s32[32]{0:T(128)}, s32[32]{0:T(128)S(1)}, u32[]{:S(2)}) copy-start(s32[32]{0:T(128)S(1)} %broadcast_multiply_fusion.3) | copy-start | bytes 388
  321.4 224.6 %copy-start.32 = (pred[32]{0:T(512)(128)(4,1)}, pred[32]{0:T(512)(128)(4,1)S(1)}, u32[]{:S(2)}) copy-start(pred[32]{0:T(512)(128)(4,1)S(1)} %fusion.204) | copy-start | bytes 100
  323.3 242.8 %copy-start.25 = (f32[32,128,4]{1,2,0:T(4,128)}, f32[32,128,4]{1,2,0:T(4,128)S(1)}, u32[]{:S(2)}) copy-start(f32[32,128,4]{1,2,0:T(4,128)S(1)} %copy.289) | copy-start | bytes 196612
  323.4 244.1 %copy-start.27 = (f32[32,128,4]{1,2,0:T(4,128)}, f32[32,128,4]{1,2,0:T(4,128)S(1)}, u32[]{:S(2)}) copy-start(f32[32,128,4]{1,2,0:T(4,128)S(1)} %copy.283) | copy-start | bytes 196612
  323.4 253.6 %copy-start.19 = (f32[32,128,4]{1,2,0:T(4,128)}, f32[32,128,4]{1,2,0:T(4,128)S(1)}, u32[]{:S(2)}) copy-start(f32[32,128,4]{1,2,0:T(4,128)S(1)} %copy.278) | copy-start | bytes 196612
  546.0 286.5 %all-gather.7.cloned.1.call-start = ((), (), s32[]{:S(2)}) async-start(), calls=%async_computation.11 | async-start | bytes 2621440 | tf_op jit(solution)/shard_map/all_gather | solution.py:161
  546.1 11.9 %copy-start.6 = (bf16[32,128,4,128]{1,3,2,0:T(8,128)(2,1)S(1)}, bf16[32,128,4,128]{1,3,2,0:T(8,128)(2,1)}, u32[]{:S(2)}) copy-start(bf16[32,128,4,128]{1,3,2,0:T(8,128)(2,1)} %copy.316) | copy-start | bytes 12582916
  608.1 27.8 %copy-start.14 = (f32[32,4,128]{2,1,0:T(4,128)S(1)}, f32[32,4,128]{2,1,0:T(4,128)}, u32[]{:S(2)}) copy-start(f32[32,4,128]{2,1,0:T(4,128)} %copy.249) | copy-start | bytes 196612
  608.1 27.8 %copy-start.15 = (f32[32,128,4]{1,2,0:T(4,128)S(1)}, f32[32,128,4]{1,2,0:T(4,128)}, u32[]{:S(2)}) copy-start(f32[32,128,4]{1,2,0:T(4,128)} %copy.256) | copy-start | bytes 196612
  608.1 27.8 %copy-start.17 = (f32[32,128,4]{1,2,0:T(4,128)S(1)}, f32[32,128,4]{1,2,0:T(4,128)}, u32[]{:S(2)}) copy-start(f32[32,128,4]{1,2,0:T(4,128)} %copy.263) | copy-start | bytes 196612
  608.1 27.8 %copy-start.20 = (f32[32,128,4]{1,2,0:T(4,128)S(1)}, f32[32,128,4]{1,2,0:T(4,128)}, u32[]{:S(2)}) copy-start(f32[32,128,4]{1,2,0:T(4,128)} %copy-done.19) | copy-start | bytes 196612
  608.1 27.8 %copy-start.21 = (f32[32,128,4]{1,2,0:T(4,128)S(1)}, f32[32,128,4]{1,2,0:T(4,128)}, u32[]{:S(2)}) copy-start(f32[32,128,4]{1,2,0:T(4,128)} %copy.273) | copy-start | bytes 196612
  608.1 27.8 %copy-start.23 = (f32[32,128,4]{1,2,0:T(4,128)S(1)}, f32[32,128,4]{1,2,0:T(4,128)}, u32[]{:S(2)}) copy-start(f32[32,128,4]{1,2,0:T(4,128)} %copy.268) | copy-start | bytes 196612
  608.1 27.8 %copy-start.26 = (f32[32,128,4]{1,2,0:T(4,128)S(1)}, f32[32,128,4]{1,2,0:T(4,128)}, u32[]{:S(2)}) copy-start(f32[32,128,4]{1,2,0:T(4,128)} %copy-done.25) | copy-start | bytes 196612
  608.1 27.8 %copy-start.28 = (f32[32,128,4]{1,2,0:T(4,128)S(1)}, f32[32,128,4]{1,2,0:T(4,128)}, u32[]{:S(2)}) copy-start(f32[32,128,4]{1,2,0:T(4,128)} %copy-done.27) | copy-start | bytes 196612
  632.4 44.0 %all-to-all-start.9 = ((bf16[4,1024,32]{1,2,0:T(8,128)(2,1)}), bf16[4,1024,32]{1,2,0:T(8,128)(2,1)S(1)}, u32[]{:S(2)}, u32[]{:S(2)}) async-start(bf16[4,1024,32]{1,2,0:T(8,128)(2,1)} %copy.342), calls=%async_computation.9 | async-start | bytes 524288 | tf_op jit(solution)/shard_map/all_to_all | solution.py:179
  676.4 97.3 %all-to-all-start.4 = ((bf16[4,1024,512]{2,1,0:T(8,128)(2,1)}), bf16[4,1024,512]{2,1,0:T(8,128)(2,1)}, u32[]{:S(2)}, u32[]{:S(2)}) async-start(bf16[4,1024,512]{2,1,0:T(8,128)(2,1)} %convert_element_type.131), calls=%async_computation.4 | async-start | bytes 8388608 | tf_op jit(solution)/shard_map/all_to_all | solution.py:175
  681.5 11.5 %copy-start.3 = (bf16[32,128,4,128]{1,3,2,0:T(8,128)(2,1)S(1)}, bf16[32,128,4,128]{1,3,2,0:T(8,128)(2,1)}, u32[]{:S(2)}) copy-start(bf16[32,128,4,128]{1,3,2,0:T(8,128)(2,1)} %copy.340) | copy-start | bytes 12582916
  681.5 11.5 %copy-start.7 = (bf16[32,128,4,128]{1,3,2,0:T(8,128)(2,1)S(1)}, bf16[32,128,4,128]{1,3,2,0:T(8,128)(2,1)}, u32[]{:S(2)}) copy-start(bf16[32,128,4,128]{1,3,2,0:T(8,128)(2,1)} %copy.316) | copy-start | bytes 12582916
  681.5 11.5 %copy-start.22 = (f32[32,128,4]{1,2,0:T(4,128)S(1)}, f32[32,128,4]{1,2,0:T(4,128)}, u32[]{:S(2)}) copy-start(f32[32,128,4]{1,2,0:T(4,128)} %copy.273) | copy-start | bytes 196612
  696.1 13.2 %copy-start.24 = (f32[32,128,4]{1,2,0:T(4,128)S(1)}, f32[32,128,4]{1,2,0:T(4,128)}, u32[]{:S(2)}) copy-start(f32[32,128,4]{1,2,0:T(4,128)} %copy.268) | copy-start | bytes 196612
  765.6 13.0 %copy-start.41 = (s32[32]{0:T(128)S(1)}, s32[32]{0:T(128)}, u32[]{:S(2)}) copy-start(s32[32]{0:T(128)} %copy-done.40) | copy-start | bytes 388
  765.6 13.0 %copy-start.43 = (s32[32]{0:T(128)S(1)}, s32[32]{0:T(128)}, u32[]{:S(2)}) copy-start(s32[32]{0:T(128)} %copy-done.42) | copy-start | bytes 388
  765.7 13.0 %copy-start.45 = (pred[32]{0:T(512)(128)(4,1)S(1)}, pred[32]{0:T(512)(128)(4,1)}, u32[]{:S(2)}) copy-start(pred[32]{0:T(512)(128)(4,1)} %copy-done.44) | copy-start | bytes 100
  773.7 119.1 %all-to-all-start.6 = ((bf16[4,1024,512]{2,1,0:T(8,128)(2,1)}), bf16[4,1024,512]{2,1,0:T(8,128)(2,1)}, u32[]{:S(2)}, u32[]{:S(2)}) async-start(bf16[4,1024,512]{2,1,0:T(8,128)(2,1)} %convert_element_type.134), calls=%async_computation.6 | async-start | bytes 8388608 | tf_op jit(solution)/shard_map/all_to_all | solution.py:176
  778.7 17.3 %copy-start.4 = (bf16[32,128,4,128]{1,3,2,0:T(8,128)(2,1)S(1)}, bf16[32,128,4,128]{1,3,2,0:T(8,128)(2,1)}, u32[]{:S(2)}) copy-start(bf16[32,128,4,128]{1,3,2,0:T(8,128)(2,1)} %copy.340) | copy-start | bytes 12582916
  778.7 17.3 %copy-start.8 = (bf16[32,128,4,128]{1,3,2,0:T(8,128)(2,1)S(1)}, bf16[32,128,4,128]{1,3,2,0:T(8,128)(2,1)}, u32[]{:S(2)}) copy-start(bf16[32,128,4,128]{1,3,2,0:T(8,128)(2,1)} %copy.316) | copy-start | bytes 12582916
  778.7 17.3 %copy-start.18 = (f32[32,128,4]{1,2,0:T(4,128)S(1)}, f32[32,128,4]{1,2,0:T(4,128)}, u32[]{:S(2)}) copy-start(f32[32,128,4]{1,2,0:T(4,128)} %copy.263) | copy-start | bytes 196612
  802.3 17.4 %copy-start.16 = (f32[32,128,4]{1,2,0:T(4,128)S(1)}, f32[32,128,4]{1,2,0:T(4,128)}, u32[]{:S(2)}) copy-start(f32[32,128,4]{1,2,0:T(4,128)} %copy.256) | copy-start | bytes 196612
  802.4 23.7 %slice-start.2 = ((s8[8388608]{0:T(1024)(128)(4,1)}), s8[4194304]{0:T(1024)(128)(4,1)S(1)}, s32[]{:S(2)}) async-start(s8[8388608]{0:T(1024)(128)(4,1)} %bitcast.313), calls=%async_computation.14 | async-start | bytes 8388608
  892.8 98.0 %all-to-all-start.7 = ((bf16[4,1024,512]{2,1,0:T(8,128)(2,1)}), bf16[4,1024,512]{2,1,0:T(8,128)(2,1)}, u32[]{:S(2)}, u32[]{:S(2)}) async-start(bf16[4,1024,512]{2,1,0:T(8,128)(2,1)} %convert_element_type.145), calls=%async_computation.7 | async-start | bytes 8388608 | tf_op jit(solution)/shard_map/all_to_all | solution.py:177
  898.3 11.1 copy-start.11
  990.8 97.6 %all-to-all-start.8 = ((bf16[4,1024,512]{2,1,0:T(8,128)(2,1)}), bf16[4,1024,512]{2,1,0:T(8,128)(2,1)}, u32[]{:S(2)}, u32[]{:S(2)}) async-start(bf16[4,1024,512]{2,1,0:T(8,128)(2,1)} %convert_element_type.147), calls=%async_computation.8 | async-start | bytes 8388608 | tf_op jit(solution)/shard_map/all_to_all | solution.py:178
  (20 other events, 113.3 us)
Sparse Core Ops, SparseCore 0:
  546.1 15.8 all-gather.4
  596.8 21.6 all-gather.6
